TPU v7x, 32 devices: a whole 2x2x4 slice. The times are simulated.
32 devices in a mesh: space: 16 (over z, y, x), mem: 2 (over core).
Axes of the slice: x: 2, y: 2, z: 4, core: 2. Of those that a mesh axis runs over, the one named last changes fastest.
Arguments:
- perturb: float32 [1024, 4096], P(('space', 'mem')), may hold values from -6 to 6
- pair_list: int32 [64, 3], P('space'), may hold values from 0 to 15, as said below
- pair_count: int32 [16], P('space'), may hold values from 1 to 4, as said below
- band_weight: float32 [8], replicated, may hold values from 0.25 to 1
- cov_scale: float32 [1], replicated, may hold values from 0.5 to 2
- target: float32 [4096, 1024], P('space', 'mem'), may hold values from -6 to 6
- first_guess: float32 [4096, 1024], P('space', 'mem'), may hold values from -6 to 6
Outputs:
- solution: float32 [4096, 1024], P('space', 'mem')
Inputs may be any that keep to these rules, and one draw needn't show every extreme that they name: `pair_list`: rows 4 * s to 4 * s + 3 are owner s's slots. The first block of each is owner s's own block s; the second is the first plus d modulo 16, with 0 <= d <= 3; each of the four pairs (d = 0 to 3) stands in exactly one slot of its owner. The third column is an index into band_weight. Only the first pair_count[s] slots of owner s are live; in every draw some owner has all 4 slots live.
All inputs are finite; a program needn't handle non-finite values.
Results may differ from a plain program's by a relative error of at most 0.0003.
Values sent between devices are 32-bit elements; how exact they have to be, the bound alone decides.
A program may use at most 64 MiB of HBM per device.

v0:
```python
import jax
import jax.numpy as jnp
from jax import lax
from jax.sharding import PartitionSpec as P

BLOCK = 256
MEMBERS = 1024
REACH_DEV = 3
NBANDS = 8
ITERS = 2


def shifted(array, axis, by):
    count = lax.axis_size(axis)
    return lax.ppermute(array, axis, [(i, (i + by) % count) for i in range(count)])


def mm(a, b, ca, cb):
    return lax.dot_general(
        a,
        b,
        (((ca,), (cb,)), ((), ())),
        precision=lax.Precision.HIGH,
        preferred_element_type=jnp.float32,
    )


def gap_weights(pair_list, pair_count, band_weight, cov_scale):
    slots = pair_list.shape[0]
    blocks_all = lax.axis_size("space")
    gap = (pair_list[:, 1] - pair_list[:, 0]) % blocks_all
    living = (jnp.arange(slots, dtype=jnp.int32) < pair_count[0]).astype(jnp.float32)
    bands = jnp.arange(NBANDS, dtype=jnp.int32)
    band_now = jnp.sum(
        jnp.where(pair_list[:, 2][:, None] == bands[None, :], band_weight[None, :], 0.0), axis=1
    )
    slot_weight = cov_scale[0] * band_now * living / (MEMBERS - 1)
    gaps = jnp.arange(REACH_DEV + 1, dtype=jnp.int32)
    return jnp.sum(jnp.where(gap[:, None] == gaps[None, :], slot_weight[:, None], 0.0), axis=0)


def per_device(perturb, pair_list, pair_count, band_weight, cov_scale, target, first_guess):
    w = gap_weights(pair_list, pair_count, band_weight, cov_scale)
    w_next = shifted(w, "space", -1)
    p0 = lax.all_to_all(perturb, "space", split_axis=1, concat_axis=0, tiled=True)
    p1 = shifted(p0, "space", -1)
    p3 = shifted(p0, "space", -3)
    x0 = first_guess
    t0 = mm(p0, p0, 0, 0) * w[0]
    t1 = mm(p0, p1, 0, 0) * w[1]
    t3 = mm(p0, p3, 0, 0) * w[3]
    t2 = mm(p1, p3, 0, 0) * w_next[2]
    t0, t1, t2, t3 = lax.psum((t0, t1, t2, t3), "mem")
    for sweep in range(ITERS):
        x1 = shifted(x0, "space", -1)
        x3 = shifted(x0, "space", -3)
        back1 = shifted(mm(t1, x0, 0, 0) + mm(t2, x3, 1, 0), "space", 1)
        back3 = shifted(mm(t3, x0, 0, 0) + mm(t2, x1, 0, 0), "space", 3)
        own = mm(t0, x0, 1, 0) + mm(t1, x1, 1, 0) + mm(t3, x3, 1, 0)
        x0 = x0 + 0.5 * (target - x0 - (own + back1 + back3))
    return x0


def solution(mesh):
    in_specs = (
        P(("space", "mem"), None),
        P("space", None),
        P("space"),
        P(),
        P(),
        P("space", "mem"),
        P("space", "mem"),
    )
    out_specs = P("space", "mem")
    return jax.shard_map(
        per_device, mesh=mesh, in_specs=in_specs, out_specs=out_specs, check_vma=False
    )
```

profile of v0, /device:TPU:2, one launch (start us, length us, event | category | flops | bytes accessed | tf_op | source)
XLA Modules:
  0.0 171.7 jit_solution(16885605686824143802)
XLA Ops:
  6.5 1.9 %copy.12 = f32[4,16,8,256]{3,2,0,1:T(8,128)} copy(f32[4,16,8,256]{3,2,1,0:T(8,128)} %bitcast.59) | data formatting | bytes 1048576 | tf_op jit(solution)/shard_map/all_to_all | solution.py:45
  8.4 7.3 %all-to-all-start = ((f32[32,16,256]{2,0,1:T(8,128)}), f32[32,16,256]{2,0,1:T(8,128)S(1)}, u32[]{:S(2)}, u32[]{:S(2)}) async-start(f32[32,16,256]{2,0,1:T(8,128)} %bitcast.52), calls=%async_computation | async-start | bytes 1048576 | tf_op jit(solution)/shard_map/all_to_all | solution.py:45
  15.7 0.0 copy-start.6
  15.7 0.0 all-reduce.3.cloned.1.call-start
  17.1 0.0 copy-done.6
  17.1 0.2 fusion.10
  17.3 0.0 copy-start.7
  17.3 0.7 copy-done.7
  18.0 0.2 select_reduce_fusion.1
  18.2 11.3 %all-to-all-done = f32[32,16,256]{2,0,1:T(8,128)S(1)} async-done(((f32[32,16,256]{2,0,1:T(8,128)}), f32[32,16,256]{2,0,1:T(8,128)S(1)}, u32[]{:S(2)}, u32[]{:S(2)}) %all-to-all-start) | async-done | bytes 524320 | tf_op jit(solution)/shard_map/all_to_all | solution.py:45
  29.5 1.5 collective-permute-start
  30.9 0.1 select_reduce_fusion
  31.0 2.6 %collective-permute-start.4 = (f32[4]{0:T(128)S(1)}, f32[4]{0:T(128)S(1)}, u32[]{:S(2)}, u32[]{:S(2)}) collective-permute-start(f32[4]{0:T(128)S(1)} %select_reduce_fusion), channel_id=1, source_target_pairs={{0,30},{2,0},{4,2},{6,4},{8,6},{10,8},{12,10},{14,12},{16,14},{18,... | collective-permute-start | bytes 56 | tf_op jit(solution)/shard_map/ppermute | solution.py:15
  33.6 1.4 collective-permute-start.2
  35.0 0.6 fusion.12
  35.6 17.6 %collective-permute-done.4 = f32[4]{0:T(128)S(1)} collective-permute-done((f32[4]{0:T(128)S(1)}, f32[4]{0:T(128)S(1)}, u32[]{:S(2)}, u32[]{:S(2)}) %collective-permute-start.4) | collective-permute-done | bytes 48 | tf_op jit(solution)/shard_map/ppermute | solution.py:15
  53.2 0.6 slice.27
  53.8 1.9 %fusion.7 = f32[256,256]{1,0:T(8,128)} fusion(f32[32,16,256]{2,0,1:T(8,128)S(1)} %all-to-all-done, f32[]{:T(128)} %bitcast.4), kind=kOutput, calls=%fused_computation.16 | convolution fusion | flops 201392128 | bytes 786436 | tf_op jit(solution)/shard_map/dot_general | solution.py:19
  55.7 0.0 collective-permute-done
  55.7 1.9 %convolution_multiply_fusion.2 = f32[256,256]{1,0:T(8,128)} fusion(f32[512,256]{1,0:T(8,128)S(1)} %bitcast.57, f32[512,256]{1,0:T(8,128)S(1)} %collective-permute-done, f32[]{:T(128)} %bitcast.7), kind=kOutput, calls=%fused_computation.19 | convolution fusion | flops 201392128 | bytes 1310724 | tf_op jit(solution)/shard_map/dot_general | solution.py:19
  57.6 0.0 collective-permute-done.2
  57.6 2.0 %convolution_multiply_fusion.1 = f32[256,256]{1,0:T(8,128)} fusion(f32[512,256]{1,0:T(8,128)S(1)} %bitcast.58, f32[512,256]{1,0:T(8,128)S(1)} %collective-permute-done.2, f32[]{:T(128)} %bitcast.8), kind=kOutput, calls=%fused_computation.18 | convolution fusion | flops 201392128 | bytes 1310724 | tf_op jit(solution)/shard_map/dot_general | solution.py:19
  59.6 1.9 %convolution_multiply_fusion = f32[256,256]{1,0:T(8,128)} fusion(f32[512,256]{1,0:T(8,128)S(1)} %collective-permute-done, f32[512,256]{1,0:T(8,128)S(1)} %collective-permute-done.2, f32[]{:T(128)} %bitcast.9), kind=kOutput, calls=%fused_computation.17 | convolution fusion | flops 201392128 | bytes 1310724 | tf_op jit(solution)/shard_map/dot_general | solution.py:19
  61.4 0.0 copy-start
  61.4 0.0 all-reduce.3.cloned.1.call-update
  61.5 1.0 copy-done
  62.5 1.8 %collective-permute-start.3 = (f32[256,512]{1,0:T(8,128)S(1)}, f32[256,512]{1,0:T(8,128)S(1)}, u32[]{:S(2)}, u32[]{:S(2)}) collective-permute-start(f32[256,512]{1,0:T(8,128)S(1)} %copy-done), channel_id=1, source_target_pairs={{0,26},{2,28},{4,30},{6,0},{8,2},{10,4},{12,6},{14,8},{16,10},{18,... | collective-permute-start | bytes 1572872 | tf_op jit(solution)/shard_map/ppermute | solution.py:15
  64.2 2.5 %collective-permute-start.1 = (f32[256,512]{1,0:T(8,128)S(1)}, f32[256,512]{1,0:T(8,128)S(1)}, u32[]{:S(2)}, u32[]{:S(2)}) collective-permute-start(f32[256,512]{1,0:T(8,128)S(1)} %copy-done), channel_id=1, source_target_pairs={{0,30},{2,0},{4,2},{6,4},{8,6},{10,8},{12,10},{14,12},{16,14},{18,... | collective-permute-start | bytes 1572872 | tf_op jit(solution)/shard_map/ppermute | solution.py:15
  66.8 14.8 %all-reduce.3.cloned.1.call-done = (f32[256,256]{1,0:T(8,128)}, f32[256,256]{1,0:T(8,128)}, f32[256,256]{1,0:T(8,128)}, f32[256,256]{1,0:T(8,128)}) async-done(((f32[256,256]{1,0:T(8,128)}, f32[256,256]{1,0:T(8,128)}, f32[256,256]{1,0:T(8,128)}, f32[256,256]{1,0:T(8,128)}), (f32[256,256]{1,0:T(8,128)}, f32[256,256]{1,0:T(8,128)}, f32[256,256]{1,0:T(8,128)}, ...) | async-done | bytes 1048592 | tf_op jit(solution)/shard_map/psum | solution.py:53
  81.6 1.4 fusion.14
  83.0 0.0 collective-permute-done.3
  83.0 0.0 copy-done.2
  83.0 0.0 copy-start.3
  83.0 0.4 convolution_add_fusion.5
  83.4 1.5 collective-permute-start.5
  85.0 0.0 copy-done.3
  85.0 0.4 fusion.15
  85.4 0.0 copy-start.5
  85.4 0.0 collective-permute-done.1
  85.4 0.4 convolution_add_fusion.4
  85.8 2.0 %collective-permute-start.6 = (f32[256,512]{1,0:T(8,128)S(1)}, f32[256,512]{1,0:T(8,128)S(1)}, u32[]{:S(2)}, u32[]{:S(2)}) collective-permute-start(f32[256,512]{1,0:T(8,128)S(1)} %convolution_add_fusion.4), channel_id=1, source_target_pairs={{0,6},{2,8},{4,10},{6,12},{8,14},{10,16},{12,18},{14,20},{16,22},{... | collective-permute-start | bytes 1572872 | tf_op jit(solution)/shard_map/ppermute | solution.py:15
  87.8 0.0 copy-done.5
  87.8 0.4 fusion.13
  88.2 0.6 copy-done.1
  88.7 0.4 convolution_add_fusion.7
  89.2 18.7 %collective-permute-done.5 = f32[256,512]{1,0:T(8,128)S(1)} collective-permute-done((f32[256,512]{1,0:T(8,128)S(1)}, f32[256,512]{1,0:T(8,128)S(1)}, u32[]{:S(2)}, u32[]{:S(2)}) %collective-permute-start.5) | collective-permute-done | bytes 524320 | tf_op jit(solution)/shard_map/ppermute | solution.py:15
  107.8 0.0 collective-permute-done.6
  107.8 0.0 copy-done.4
  107.8 0.5 fusion.6
  108.3 6.2 %collective-permute-start.8 = (f32[256,512]{1,0:T(8,128)S(1)}, f32[256,512]{1,0:T(8,128)S(1)}, u32[]{:S(2)}, u32[]{:S(2)}) collective-permute-start(f32[256,512]{1,0:T(8,128)S(1)} %fusion.6), channel_id=1, source_target_pairs={{0,26},{2,28},{4,30},{6,0},{8,2},{10,4},{12,6},{14,8},{16,10},{18,... | collective-permute-start | bytes 1572872 | tf_op jit(solution)/shard_map/ppermute | solution.py:15
  114.5 0.0 collective-permute-start.7
  114.5 10.8 %collective-permute-done.8 = f32[256,512]{1,0:T(8,128)S(1)} collective-permute-done((f32[256,512]{1,0:T(8,128)S(1)}, f32[256,512]{1,0:T(8,128)S(1)}, u32[]{:S(2)}, u32[]{:S(2)}) %collective-permute-start.8) | collective-permute-done | bytes 524320 | tf_op jit(solution)/shard_map/ppermute | solution.py:15
  125.3 0.4 fusion.17
  125.7 0.4 convolution_add_fusion.1
  126.1 3.4 %collective-permute-start.9 = (f32[256,512]{1,0:T(8,128)S(1)}, f32[256,512]{1,0:T(8,128)S(1)}, u32[]{:S(2)}, u32[]{:S(2)}) collective-permute-start(f32[256,512]{1,0:T(8,128)S(1)} %convolution_add_fusion.1), channel_id=1, source_target_pairs={{0,2},{2,4},{4,6},{6,8},{8,10},{10,12},{12,14},{14,16},{16,18},{18... | collective-permute-start | bytes 1572872 | tf_op jit(solution)/shard_map/ppermute | solution.py:15
  129.5 7.0 %collective-permute-done.7 = f32[256,512]{1,0:T(8,128)S(1)} collective-permute-done((f32[256,512]{1,0:T(8,128)S(1)}, f32[256,512]{1,0:T(8,128)S(1)}, u32[]{:S(2)}, u32[]{:S(2)}) %collective-permute-start.7) | collective-permute-done | bytes 524320 | tf_op jit(solution)/shard_map/ppermute | solution.py:15
  136.5 0.4 fusion.18
  136.9 0.4 convolution_add_fusion
  137.3 1.7 %collective-permute-start.10 = (f32[256,512]{1,0:T(8,128)S(1)}, f32[256,512]{1,0:T(8,128)S(1)}, u32[]{:S(2)}, u32[]{:S(2)}) collective-permute-start(f32[256,512]{1,0:T(8,128)S(1)} %convolution_add_fusion), channel_id=1, source_target_pairs={{0,6},{2,8},{4,10},{6,12},{8,14},{10,16},{12,18},{14,20},{16,22},{... | collective-permute-start | bytes 1572872 | tf_op jit(solution)/shard_map/ppermute | solution.py:15
  139.1 0.4 fusion.16
  139.5 0.4 convolution_add_fusion.3
  139.9 18.9 %collective-permute-done.9 = f32[256,512]{1,0:T(8,128)S(1)} collective-permute-done((f32[256,512]{1,0:T(8,128)S(1)}, f32[256,512]{1,0:T(8,128)S(1)}, u32[]{:S(2)}, u32[]{:S(2)}) %collective-permute-start.9) | collective-permute-done | bytes 524320 | tf_op jit(solution)/shard_map/ppermute | solution.py:15
  158.8 4.7 %collective-permute-done.10 = f32[256,512]{1,0:T(8,128)S(1)} collective-permute-done((f32[256,512]{1,0:T(8,128)S(1)}, f32[256,512]{1,0:T(8,128)S(1)}, u32[]{:S(2)}, u32[]{:S(2)}) %collective-permute-start.10) | collective-permute-done | bytes 524320 | tf_op jit(solution)/shard_map/ppermute | solution.py:15
  163.6 1.3 multiply_add_fusion
  (4 shorter events, 0.0 us)
Async XLA Ops:
  8.4 21.0 %all-to-all-start = ((f32[32,16,256]{2,0,1:T(8,128)}), f32[32,16,256]{2,0,1:T(8,128)S(1)}, u32[]{:S(2)}, u32[]{:S(2)}) async-start(f32[32,16,256]{2,0,1:T(8,128)} %bitcast.52), calls=%async_computation | async-start | bytes 1048576 | tf_op jit(solution)/shard_map/all_to_all | solution.py:45
  15.7 1.4 copy-start.6
  15.7 65.8 %all-reduce.3.cloned.1.call-start = ((), (), s32[]{:S(2)}) async-start(), calls=%async_computation.1 | async-start | bytes 2097152 | tf_op jit(solution)/shard_map/psum | solution.py:53
  17.3 0.7 copy-start.7
  29.5 26.3 %collective-permute-start = (f32[512,256]{1,0:T(8,128)S(1)}, f32[512,256]{1,0:T(8,128)S(1)}, u32[]{:S(2)}, u32[]{:S(2)}) collective-permute-start(f32[512,256]{1,0:T(8,128)S(1)} %bitcast.55), channel_id=1, source_target_pairs={{0,30},{2,0},{4,2},{6,4},{8,6},{10,8},{12,10},{14,12},{16,14},{18,... | collective-permute-start | bytes 1572872 | tf_op jit(solution)/shard_map/ppermute | solution.py:15
  31.0 22.2 %collective-permute-start.4 = (f32[4]{0:T(128)S(1)}, f32[4]{0:T(128)S(1)}, u32[]{:S(2)}, u32[]{:S(2)}) collective-permute-start(f32[4]{0:T(128)S(1)} %select_reduce_fusion), channel_id=1, source_target_pairs={{0,30},{2,0},{4,2},{6,4},{8,6},{10,8},{12,10},{14,12},{16,14},{18,... | collective-permute-start | bytes 56 | tf_op jit(solution)/shard_map/ppermute | solution.py:15
  33.6 24.0 %collective-permute-start.2 = (f32[512,256]{1,0:T(8,128)S(1)}, f32[512,256]{1,0:T(8,128)S(1)}, u32[]{:S(2)}, u32[]{:S(2)}) collective-permute-start(f32[512,256]{1,0:T(8,128)S(1)} %bitcast.56), channel_id=1, source_target_pairs={{0,26},{2,28},{4,30},{6,0},{8,2},{10,4},{12,6},{14,8},{16,10},{18,... | collective-permute-start | bytes 1572872 | tf_op jit(solution)/shard_map/ppermute | solution.py:15
  61.4 1.0 copy-start
  62.5 20.5 %collective-permute-start.3 = (f32[256,512]{1,0:T(8,128)S(1)}, f32[256,512]{1,0:T(8,128)S(1)}, u32[]{:S(2)}, u32[]{:S(2)}) collective-permute-start(f32[256,512]{1,0:T(8,128)S(1)} %copy-done), channel_id=1, source_target_pairs={{0,26},{2,28},{4,30},{6,0},{8,2},{10,4},{12,6},{14,8},{16,10},{18,... | collective-permute-start | bytes 1572872 | tf_op jit(solution)/shard_map/ppermute | solution.py:15
  64.2 21.1 %collective-permute-start.1 = (f32[256,512]{1,0:T(8,128)S(1)}, f32[256,512]{1,0:T(8,128)S(1)}, u32[]{:S(2)}, u32[]{:S(2)}) collective-permute-start(f32[256,512]{1,0:T(8,128)S(1)} %copy-done), channel_id=1, source_target_pairs={{0,30},{2,0},{4,2},{6,4},{8,6},{10,8},{12,10},{14,12},{16,14},{18,... | collective-permute-start | bytes 1572872 | tf_op jit(solution)/shard_map/ppermute | solution.py:15
  81.6 1.4 copy-start.2
  83.0 1.9 %copy-start.3 = (f32[256,256]{1,0:T(8,128)S(1)}, f32[256,256]{1,0:T(8,128)}, u32[]{:S(2)}) copy-start(f32[256,256]{1,0:T(8,128)} %get-tuple-element.7) | copy-start | bytes 786436
  83.4 24.4 %collective-permute-start.5 = (f32[256,512]{1,0:T(8,128)S(1)}, f32[256,512]{1,0:T(8,128)S(1)}, u32[]{:S(2)}, u32[]{:S(2)}) collective-permute-start(f32[256,512]{1,0:T(8,128)S(1)} %convolution_add_fusion.5), channel_id=1, source_target_pairs={{0,2},{2,4},{4,6},{6,8},{8,10},{10,12},{12,14},{14,16},{16,18},{18... | collective-permute-start | bytes 1572872 | tf_op jit(solution)/shard_map/ppermute | solution.py:15
  85.4 2.4 %copy-start.5 = (f32[256,256]{1,0:T(8,128)S(1)}, f32[256,256]{1,0:T(8,128)}, u32[]{:S(2)}) copy-start(f32[256,256]{1,0:T(8,128)} %get-tuple-element.10) | copy-start | bytes 786436
  85.8 22.0 %collective-permute-start.6 = (f32[256,512]{1,0:T(8,128)S(1)}, f32[256,512]{1,0:T(8,128)S(1)}, u32[]{:S(2)}, u32[]{:S(2)}) collective-permute-start(f32[256,512]{1,0:T(8,128)S(1)} %convolution_add_fusion.4), channel_id=1, source_target_pairs={{0,6},{2,8},{4,10},{6,12},{8,14},{10,16},{12,18},{14,20},{16,22},{... | collective-permute-start | bytes 1572872 | tf_op jit(solution)/shard_map/ppermute | solution.py:15
  87.8 1.0 copy-start.1
  88.7 19.1 %copy-start.4 = (f32[256,512]{1,0:T(8,128)S(1)}, f32[256,512]{1,0:T(8,128)}, u32[]{:S(2)}) copy-start(f32[256,512]{1,0:T(8,128)} %param.12) | copy-start | bytes 1572868
  108.3 17.0 %collective-permute-start.8 = (f32[256,512]{1,0:T(8,128)S(1)}, f32[256,512]{1,0:T(8,128)S(1)}, u32[]{:S(2)}, u32[]{:S(2)}) collective-permute-start(f32[256,512]{1,0:T(8,128)S(1)} %fusion.6), channel_id=1, source_target_pairs={{0,26},{2,28},{4,30},{6,0},{8,2},{10,4},{12,6},{14,8},{16,10},{18,... | collective-permute-start | bytes 1572872 | tf_op jit(solution)/shard_map/ppermute | solution.py:15
  114.5 21.9 %collective-permute-start.7 = (f32[256,512]{1,0:T(8,128)S(1)}, f32[256,512]{1,0:T(8,128)S(1)}, u32[]{:S(2)}, u32[]{:S(2)}) collective-permute-start(f32[256,512]{1,0:T(8,128)S(1)} %fusion.6), channel_id=1, source_target_pairs={{0,30},{2,0},{4,2},{6,4},{8,6},{10,8},{12,10},{14,12},{16,14},{18,... | collective-permute-start | bytes 1572872 | tf_op jit(solution)/shard_map/ppermute | solution.py:15
  126.1 32.7 %collective-permute-start.9 = (f32[256,512]{1,0:T(8,128)S(1)}, f32[256,512]{1,0:T(8,128)S(1)}, u32[]{:S(2)}, u32[]{:S(2)}) collective-permute-start(f32[256,512]{1,0:T(8,128)S(1)} %convolution_add_fusion.1), channel_id=1, source_target_pairs={{0,2},{2,4},{4,6},{6,8},{8,10},{10,12},{12,14},{14,16},{16,18},{18... | collective-permute-start | bytes 1572872 | tf_op jit(solution)/shard_map/ppermute | solution.py:15
  137.3 26.2 %collective-permute-start.10 = (f32[256,512]{1,0:T(8,128)S(1)}, f32[256,512]{1,0:T(8,128)S(1)}, u32[]{:S(2)}, u32[]{:S(2)}) collective-permute-start(f32[256,512]{1,0:T(8,128)S(1)} %convolution_add_fusion), channel_id=1, source_target_pairs={{0,6},{2,8},{4,10},{6,12},{8,14},{10,16},{12,18},{14,20},{16,22},{... | collective-permute-start | bytes 1572872 | tf_op jit(solution)/shard_map/ppermute | solution.py:15
Sparse Core Ops, SparseCore 0:
  61.6 19.9 all-reduce.2
where the time goes:
time: 172 us
  waiting for transfers between devices  104 us (60%)
  starting transfers between devices  31.9 us (19%)
  matrix products  15.3 us (9%)
  between operations  14.9 us (9%)
  local copies, waits for them, and re-layouts  5.37 us (3%)
    ppermute x11, waiting for transfers between devices, shifted(): lax.ppermute(array, axis, [(i, (i + by) % count) for i in range(count)])  77.7 us
    ppermute x11, starting transfers between devices, shifted(): lax.ppermute(array, axis, [(i, (i + by) % count) for i in range(count)])  24.6 us
    dot_general x18, matrix products, mm(): lax.dot_general(a, b, (((ca,), (cb,)), ((), ())), precision=lax.Precision...  15.3 us
    psum x1, waiting for transfers between devices, per_device(): t0, t1, t2, t3 = lax.psum((t0, t1, t2, t3), 'mem')  14.8 us
    all_to_all x1, waiting for transfers between devices, per_device(): lax.all_to_all(perturb, 'space', split_axis=1, concat_axis=0, tiled=True)  11.3 us
    all_to_all x1, starting transfers between devices, per_device(): lax.all_to_all(perturb, 'space', split_axis=1, concat_axis=0, tiled=True)  7.31 us
  transfers between devices with their start and end apart: 13, of which 8 were waited for; matrix products, arithmetic and copies ran while one was open for 7% of the time, Pallas kernels for 0%

commit v1 on v0

--- a/solution.py
+++ b/solution.py
@@ -8,6 +8,19 @@
 REACH_DEV = 3
 NBANDS = 8
 ITERS = 2
+
+
+def set_series(load, array_axis, inputs):
+    current_block, arr_now = (load.shape[:array_axis], load.shape[array_axis + 1 :])
+    val2 = jnp.moveaxis(load.reshape(*current_block, inputs, -1, *arr_now), array_axis, 0)
+    return val2
+
+
+def deliver_digits(vec, join_dim):
+    field_out = list(vec.shape[1:])
+    field_out[join_dim] *= vec.shape[0]
+    z_new = jnp.moveaxis(vec, 0, join_dim).reshape(field_out)
+    return z_new
 
 
 def shifted(array, axis, by):
@@ -42,7 +55,19 @@
 def per_device(perturb, pair_list, pair_count, band_weight, cov_scale, target, first_guess):
     w = gap_weights(pair_list, pair_count, band_weight, cov_scale)
     w_next = shifted(w, "space", -1)
-    p0 = lax.all_to_all(perturb, "space", split_axis=1, concat_axis=0, tiled=True)
+    local_now, placed = (lax.axis_size("space"), lax.axis_index("space"))
+    oldest = set_series(perturb, 1, local_now)
+    taken_in = oldest
+    for j in [*range(1, local_now)]:
+        f_now, h_now = ((placed + j) % local_now, (placed - j) % local_now)
+        part_next = lax.dynamic_index_in_dim(oldest, f_now, 0)
+        earlier = lax.ppermute(
+            part_next,
+            axis_name="space",
+            perm=tuple(((pp, (pp + j) % local_now) for pp in range(local_now))),
+        )
+        taken_in = lax.dynamic_update_slice_in_dim(taken_in, earlier, h_now, axis=0)
+    p0 = deliver_digits(taken_in, 0)
     p1 = shifted(p0, "space", -1)
     p3 = shifted(p0, "space", -3)
     x0 = first_guess

time: 172 us -> 181 us (1.052)
  the two profiles are of different devices: /device:TPU:2 before, /device:TPU:4 now
where the time goes in v1:
time: 181 us
  waiting for transfers between devices  98.7 us (55%)
  starting transfers between devices  46.2 us (26%)
  between operations  15.5 us (9%)
  matrix products  15.4 us (9%)
  local copies, waits for them, and re-layouts  4.79 us (3%)
    ppermute x11, waiting for transfers between devices, shifted(): lax.ppermute(array, axis, [(i, (i + by) % count) for i in range(count)])  81.5 us
    ppermute x15, starting transfers between devices, per_device(): lax.ppermute(part_next, axis_name='space', perm=tuple(((pp, (pp + j) % lo...  28.1 us
    ppermute x11, starting transfers between devices, shifted(): lax.ppermute(array, axis, [(i, (i + by) % count) for i in range(count)])  18.1 us
    psum x1, waiting for transfers between devices, per_device(): t0, t1, t2, t3 = lax.psum((t0, t1, t2, t3), 'mem')  15.4 us
    dot_general x18, matrix products, mm(): lax.dot_general(a, b, (((ca,), (cb,)), ((), ())), precision=lax.Precision...  15.4 us
  transfers between devices with their start and end apart: 27, of which 10 were waited for; matrix products, arithmetic and copies ran while one was open for 6% of the time, Pallas kernels for 0%

profile of v1, /device:TPU:4, one launch (start us, length us, event | category | flops | bytes accessed | tf_op | source)
XLA Modules:
  0.0 181.0 jit_solution(12974716263955950814)
XLA Ops:
  6.5 1.2 copy.26
  7.8 0.6 constant_dynamic-slice_fusion
  8.4 1.5 collective-permute-start
  10.0 1.5 collective-permute-start.1
  11.5 2.4 %collective-permute-start.2 = (f32[1,32,256]{2,1,0:T(8,128)S(1)}, f32[1,32,256]{2,1,0:T(8,128)S(1)}, u32[]{:S(2)}, u32[]{:S(2)}) collective-permute-start(f32[1,32,256]{2,1,0:T(8,128)S(1)} %bitcast.113), channel_id=1, source_target_pairs={{0,6},{2,8},{4,10},{6,12},{8,14},{10,16},{12,18},{14,20},{16,22},{... | collective-permute-start | bytes 98312 | tf_op jit(solution)/shard_map/ppermute | solution.py:64
  14.0 1.6 collective-permute-start.3
  15.5 0.3 collective-permute-start.4
  15.8 0.2 fusion.9
  16.0 0.2 select_reduce_fusion.1
  18.1 2.6 %collective-permute-start.5 = (f32[1,32,256]{2,1,0:T(8,128)S(1)}, f32[1,32,256]{2,1,0:T(8,128)S(1)}, u32[]{:S(2)}, u32[]{:S(2)}) collective-permute-start(f32[1,32,256]{2,1,0:T(8,128)S(1)} %bitcast.125), channel_id=1, source_target_pairs={{0,12},{2,14},{4,16},{6,18},{8,20},{10,22},{12,24},{14,26},{16,28}... | collective-permute-start | bytes 98312 | tf_op jit(solution)/shard_map/ppermute | solution.py:64
  20.7 3.5 %collective-permute-start.6 = (f32[1,32,256]{2,1,0:T(8,128)S(1)}, f32[1,32,256]{2,1,0:T(8,128)S(1)}, u32[]{:S(2)}, u32[]{:S(2)}) collective-permute-start(f32[1,32,256]{2,1,0:T(8,128)S(1)} %bitcast.124), channel_id=1, source_target_pairs={{0,14},{2,16},{4,18},{6,20},{8,22},{10,24},{12,26},{14,28},{16,30}... | collective-permute-start | bytes 98312 | tf_op jit(solution)/shard_map/ppermute | solution.py:64
  24.2 1.3 collective-permute-start.7
  25.5 0.9 collective-permute-start.8
  26.4 2.2 %collective-permute-start.9 = (f32[1,32,256]{2,1,0:T(8,128)S(1)}, f32[1,32,256]{2,1,0:T(8,128)S(1)}, u32[]{:S(2)}, u32[]{:S(2)}) collective-permute-start(f32[1,32,256]{2,1,0:T(8,128)S(1)} %bitcast.121), channel_id=1, source_target_pairs={{0,20},{2,22},{4,24},{6,26},{8,28},{10,30},{12,0},{14,2},{16,4},{1... | collective-permute-start | bytes 98312 | tf_op jit(solution)/shard_map/ppermute | solution.py:64
  28.6 3.2 %collective-permute-start.10 = (f32[1,32,256]{2,1,0:T(8,128)S(1)}, f32[1,32,256]{2,1,0:T(8,128)S(1)}, u32[]{:S(2)}, u32[]{:S(2)}) collective-permute-start(f32[1,32,256]{2,1,0:T(8,128)S(1)} %bitcast.120), channel_id=1, source_target_pairs={{0,22},{2,24},{4,26},{6,28},{8,30},{10,0},{12,2},{14,4},{16,6},{18... | collective-permute-start | bytes 98312 | tf_op jit(solution)/shard_map/ppermute | solution.py:64
  31.8 2.0 %collective-permute-start.11 = (f32[1,32,256]{2,1,0:T(8,128)S(1)}, f32[1,32,256]{2,1,0:T(8,128)S(1)}, u32[]{:S(2)}, u32[]{:S(2)}) collective-permute-start(f32[1,32,256]{2,1,0:T(8,128)S(1)} %bitcast.119), channel_id=1, source_target_pairs={{0,24},{2,26},{4,28},{6,30},{8,0},{10,2},{12,4},{14,6},{16,8},{18,... | collective-permute-start | bytes 98312 | tf_op jit(solution)/shard_map/ppermute | solution.py:64
  33.8 0.1 collective-permute-start.12
  33.9 1.3 collective-permute-start.13
  35.2 3.7 %collective-permute-start.14 = (f32[1,32,256]{2,1,0:T(8,128)S(1)}, f32[1,32,256]{2,1,0:T(8,128)S(1)}, u32[]{:S(2)}, u32[]{:S(2)}) collective-permute-start(f32[1,32,256]{2,1,0:T(8,128)S(1)} %bitcast.116), channel_id=1, source_target_pairs={{0,30},{2,0},{4,2},{6,4},{8,6},{10,8},{12,10},{14,12},{16,14},{18,... | collective-permute-start | bytes 98312 | tf_op jit(solution)/shard_map/ppermute | solution.py:64
  39.0 0.6 collective-permute-done.12
  39.6 1.1 collective-permute-done.14
  40.7 3.4 %collective-permute-start.15 = (f32[512,256]{1,0:T(8,128)S(1)}, f32[512,256]{1,0:T(8,128)S(1)}, u32[]{:S(2)}, u32[]{:S(2)}) collective-permute-start(f32[512,256]{1,0:T(8,128)S(1)} %bitcast.104), channel_id=1, source_target_pairs={{0,30},{2,0},{4,2},{6,4},{8,6},{10,8},{12,10},{14,12},{16,14},{18,... | collective-permute-start | bytes 1572872 | tf_op jit(solution)/shard_map/ppermute | solution.py:28
  44.1 0.1 select_reduce_fusion
  44.2 0.0 collective-permute-start.19
  44.2 2.4 %collective-permute-start.17 = (f32[512,256]{1,0:T(8,128)S(1)}, f32[512,256]{1,0:T(8,128)S(1)}, u32[]{:S(2)}, u32[]{:S(2)}) collective-permute-start(f32[512,256]{1,0:T(8,128)S(1)} %bitcast.105), channel_id=1, source_target_pairs={{0,26},{2,28},{4,30},{6,0},{8,2},{10,4},{12,6},{14,8},{16,10},{18,... | collective-permute-start | bytes 1572872 | tf_op jit(solution)/shard_map/ppermute | solution.py:28
  46.5 0.7 fusion.11
  47.2 14.6 %collective-permute-done.19 = f32[4]{0:T(128)S(1)} collective-permute-done((f32[4]{0:T(128)S(1)}, f32[4]{0:T(128)S(1)}, u32[]{:S(2)}, u32[]{:S(2)}) %collective-permute-start.19) | collective-permute-done | bytes 48 | tf_op jit(solution)/shard_map/ppermute | solution.py:28
  61.8 0.6 slice.27
  62.4 1.9 %fusion.7 = f32[256,256]{1,0:T(8,128)} fusion(f32[16,32,256]{2,1,0:T(8,128)S(1)} %constant_dynamic-update-slice_fusion, f32[]{:T(128)} %bitcast.4), kind=kOutput, calls=%fused_computation.16 | convolution fusion | flops 201392128 | bytes 786436 | tf_op jit(solution)/shard_map/dot_general | solution.py:32
  64.3 1.9 %convolution_multiply_fusion.2 = f32[256,256]{1,0:T(8,128)} fusion(f32[512,256]{1,0:T(8,128)S(1)} %bitcast.106, f32[512,256]{1,0:T(8,128)S(1)} %collective-permute-done.15, f32[]{:T(128)} %bitcast.6), kind=kOutput, calls=%fused_computation.19 | convolution fusion | flops 201392128 | bytes 1310724 | tf_op jit(solution)/shard_map/dot_general | solution.py:32
  66.2 1.9 %convolution_multiply_fusion = f32[256,256]{1,0:T(8,128)} fusion(f32[512,256]{1,0:T(8,128)S(1)} %collective-permute-done.15, f32[512,256]{1,0:T(8,128)S(1)} %collective-permute-done.17, f32[]{:T(128)} %bitcast.8), kind=kOutput, calls=%fused_computation.17 | convolution fusion | flops 201392128 | bytes 1310724 | tf_op jit(solution)/shard_map/dot_general | solution.py:32
  68.0 2.0 %convolution_multiply_fusion.1 = f32[256,256]{1,0:T(8,128)} fusion(f32[512,256]{1,0:T(8,128)S(1)} %bitcast.107, f32[512,256]{1,0:T(8,128)S(1)} %collective-permute-done.17, f32[]{:T(128)} %bitcast.7), kind=kOutput, calls=%fused_computation.18 | convolution fusion | flops 201392128 | bytes 1310724 | tf_op jit(solution)/shard_map/dot_general | solution.py:32
  70.1 1.0 copy-done
  71.1 2.8 %collective-permute-start.18 = (f32[256,512]{1,0:T(8,128)S(1)}, f32[256,512]{1,0:T(8,128)S(1)}, u32[]{:S(2)}, u32[]{:S(2)}) collective-permute-start(f32[256,512]{1,0:T(8,128)S(1)} %copy-done), channel_id=1, source_target_pairs={{0,26},{2,28},{4,30},{6,0},{8,2},{10,4},{12,6},{14,8},{16,10},{18,... | collective-permute-start | bytes 1572872 | tf_op jit(solution)/shard_map/ppermute | solution.py:28
  73.9 0.6 collective-permute-start.16
  74.5 15.4 %all-reduce.3.cloned.1.call-done = (f32[256,256]{1,0:T(8,128)}, f32[256,256]{1,0:T(8,128)}, f32[256,256]{1,0:T(8,128)}, f32[256,256]{1,0:T(8,128)}) async-done(((f32[256,256]{1,0:T(8,128)}, f32[256,256]{1,0:T(8,128)}, f32[256,256]{1,0:T(8,128)}, f32[256,256]{1,0:T(8,128)}), (f32[256,256]{1,0:T(8,128)}, f32[256,256]{1,0:T(8,128)}, f32[256,256]{1,0:T(8,128)}, ...) | async-done | bytes 1048592 | tf_op jit(solution)/shard_map/psum | solution.py:78
  89.9 1.4 fusion.13
  91.4 0.4 convolution_add_fusion.5
  91.8 1.5 collective-permute-start.20
  93.3 0.4 fusion.14
  93.7 0.1 collective-permute-done.16
  93.8 0.4 convolution_add_fusion.4
  94.2 2.4 %collective-permute-start.21 = (f32[256,512]{1,0:T(8,128)S(1)}, f32[256,512]{1,0:T(8,128)S(1)}, u32[]{:S(2)}, u32[]{:S(2)}) collective-permute-start(f32[256,512]{1,0:T(8,128)S(1)} %convolution_add_fusion.4), channel_id=1, source_target_pairs={{0,6},{2,8},{4,10},{6,12},{8,14},{10,16},{12,18},{14,20},{16,22},{... | collective-permute-start | bytes 1572872 | tf_op jit(solution)/shard_map/ppermute | solution.py:28
  96.6 0.4 fusion.12
  97.0 0.6 copy-done.1
  97.6 0.4 convolution_add_fusion.7
  98.0 20.2 %collective-permute-done.20 = f32[256,512]{1,0:T(8,128)S(1)} collective-permute-done((f32[256,512]{1,0:T(8,128)S(1)}, f32[256,512]{1,0:T(8,128)S(1)}, u32[]{:S(2)}, u32[]{:S(2)}) %collective-permute-start.20) | collective-permute-done | bytes 524320 | tf_op jit(solution)/shard_map/ppermute | solution.py:28
  118.1 1.5 collective-permute-done.21
  119.7 0.5 fusion.6
  120.2 1.8 collective-permute-start.23
  122.0 2.4 %collective-permute-start.22 = (f32[256,512]{1,0:T(8,128)S(1)}, f32[256,512]{1,0:T(8,128)S(1)}, u32[]{:S(2)}, u32[]{:S(2)}) collective-permute-start(f32[256,512]{1,0:T(8,128)S(1)} %fusion.6), channel_id=1, source_target_pairs={{0,30},{2,0},{4,2},{6,4},{8,6},{10,8},{12,10},{14,12},{16,14},{18,... | collective-permute-start | bytes 1572872 | tf_op jit(solution)/shard_map/ppermute | solution.py:28
  124.3 11.2 %collective-permute-done.23 = f32[256,512]{1,0:T(8,128)S(1)} collective-permute-done((f32[256,512]{1,0:T(8,128)S(1)}, f32[256,512]{1,0:T(8,128)S(1)}, u32[]{:S(2)}, u32[]{:S(2)}) %collective-permute-start.23) | collective-permute-done | bytes 524320 | tf_op jit(solution)/shard_map/ppermute | solution.py:28
  135.5 0.4 fusion.16
  135.9 0.4 convolution_add_fusion.1
  136.3 0.8 collective-permute-start.24
  137.1 18.9 %collective-permute-done.22 = f32[256,512]{1,0:T(8,128)S(1)} collective-permute-done((f32[256,512]{1,0:T(8,128)S(1)}, f32[256,512]{1,0:T(8,128)S(1)}, u32[]{:S(2)}, u32[]{:S(2)}) %collective-permute-start.22) | collective-permute-done | bytes 524320 | tf_op jit(solution)/shard_map/ppermute | solution.py:28
  155.9 0.4 fusion.17
  156.4 0.4 convolution_add_fusion
  156.8 0.1 collective-permute-start.25
  156.9 0.4 fusion.15
  157.3 0.4 convolution_add_fusion.3
  157.7 11.4 %collective-permute-done.24 = f32[256,512]{1,0:T(8,128)S(1)} collective-permute-done((f32[256,512]{1,0:T(8,128)S(1)}, f32[256,512]{1,0:T(8,128)S(1)}, u32[]{:S(2)}, u32[]{:S(2)}) %collective-permute-start.24) | collective-permute-done | bytes 524320 | tf_op jit(solution)/shard_map/ppermute | solution.py:28
  169.1 3.8 %collective-permute-done.25 = f32[256,512]{1,0:T(8,128)S(1)} collective-permute-done((f32[256,512]{1,0:T(8,128)S(1)}, f32[256,512]{1,0:T(8,128)S(1)}, u32[]{:S(2)}, u32[]{:S(2)}) %collective-permute-start.25) | collective-permute-done | bytes 524320 | tf_op jit(solution)/shard_map/ppermute | solution.py:28
  172.9 1.3 multiply_add_fusion
  (66 shorter events, 0.3 us)
Async XLA Ops:
  6.5 83.4 %all-reduce.3.cloned.1.call-start = ((), (), s32[]{:S(2)}) async-start(), calls=%async_computation | async-start | bytes 2097152 | tf_op jit(solution)/shard_map/psum | solution.py:78
  7.8 8.0 %copy-start.7 = (s32[4,3]{1,0:T(4,128)S(1)}, s32[4,3]{1,0:T(4,128)}, u32[]{:S(2)}) copy-start(s32[4,3]{1,0:T(4,128)} %param.8) | copy-start | bytes 148
  7.8 8.2 %copy-start.8 = (f32[8]{0:T(128)S(1)}, f32[8]{0:T(128)}, u32[]{:S(2)}) copy-start(f32[8]{0:T(128)} %param.10) | copy-start | bytes 100
  8.4 8.1 %copy-start.5 = (f32[32,4096]{1,0:T(8,128)S(1)}, f32[32,4096]{1,0:T(8,128)}, u32[]{:S(2)}) copy-start(f32[32,4096]{1,0:T(8,128)} %param.7) | copy-start | bytes 1572868
  8.4 9.6 %collective-permute-start = (f32[1,32,256]{2,1,0:T(8,128)S(1)}, f32[1,32,256]{2,1,0:T(8,128)S(1)}, u32[]{:S(2)}, u32[]{:S(2)}) collective-permute-start(f32[1,32,256]{2,1,0:T(8,128)S(1)} %bitcast.115), channel_id=1, source_target_pairs={{0,2},{2,4},{4,6},{6,8},{8,10},{10,12},{12,14},{14,16},{16,18},{18... | collective-permute-start | bytes 98312 | tf_op jit(solution)/shard_map/ppermute | solution.py:64
  10.0 10.7 %collective-permute-start.1 = (f32[1,32,256]{2,1,0:T(8,128)S(1)}, f32[1,32,256]{2,1,0:T(8,128)S(1)}, u32[]{:S(2)}, u32[]{:S(2)}) collective-permute-start(f32[1,32,256]{2,1,0:T(8,128)S(1)} %bitcast.114), channel_id=1, source_target_pairs={{0,4},{2,6},{4,8},{6,10},{8,12},{10,14},{12,16},{14,18},{16,20},{1... | collective-permute-start | bytes 98312 | tf_op jit(solution)/shard_map/ppermute | solution.py:64
  11.5 12.7 %collective-permute-start.2 = (f32[1,32,256]{2,1,0:T(8,128)S(1)}, f32[1,32,256]{2,1,0:T(8,128)S(1)}, u32[]{:S(2)}, u32[]{:S(2)}) collective-permute-start(f32[1,32,256]{2,1,0:T(8,128)S(1)} %bitcast.113), channel_id=1, source_target_pairs={{0,6},{2,8},{4,10},{6,12},{8,14},{10,16},{12,18},{14,20},{16,22},{... | collective-permute-start | bytes 98312 | tf_op jit(solution)/shard_map/ppermute | solution.py:64
  14.0 11.5 %collective-permute-start.3 = (f32[1,32,256]{2,1,0:T(8,128)S(1)}, f32[1,32,256]{2,1,0:T(8,128)S(1)}, u32[]{:S(2)}, u32[]{:S(2)}) collective-permute-start(f32[1,32,256]{2,1,0:T(8,128)S(1)} %bitcast.112), channel_id=1, source_target_pairs={{0,8},{2,10},{4,12},{6,14},{8,16},{10,18},{12,20},{14,22},{16,24},... | collective-permute-start | bytes 98312 | tf_op jit(solution)/shard_map/ppermute | solution.py:64
  15.5 10.8 %collective-permute-start.4 = (f32[1,32,256]{2,1,0:T(8,128)S(1)}, f32[1,32,256]{2,1,0:T(8,128)S(1)}, u32[]{:S(2)}, u32[]{:S(2)}) collective-permute-start(f32[1,32,256]{2,1,0:T(8,128)S(1)} %bitcast.111), channel_id=1, source_target_pairs={{0,10},{2,12},{4,14},{6,16},{8,18},{10,20},{12,22},{14,24},{16,26}... | collective-permute-start | bytes 98312 | tf_op jit(solution)/shard_map/ppermute | solution.py:64
  18.1 10.5 %collective-permute-start.5 = (f32[1,32,256]{2,1,0:T(8,128)S(1)}, f32[1,32,256]{2,1,0:T(8,128)S(1)}, u32[]{:S(2)}, u32[]{:S(2)}) collective-permute-start(f32[1,32,256]{2,1,0:T(8,128)S(1)} %bitcast.125), channel_id=1, source_target_pairs={{0,12},{2,14},{4,16},{6,18},{8,20},{10,22},{12,24},{14,26},{16,28}... | collective-permute-start | bytes 98312 | tf_op jit(solution)/shard_map/ppermute | solution.py:64
  20.7 11.1 %collective-permute-start.6 = (f32[1,32,256]{2,1,0:T(8,128)S(1)}, f32[1,32,256]{2,1,0:T(8,128)S(1)}, u32[]{:S(2)}, u32[]{:S(2)}) collective-permute-start(f32[1,32,256]{2,1,0:T(8,128)S(1)} %bitcast.124), channel_id=1, source_target_pairs={{0,14},{2,16},{4,18},{6,20},{8,22},{10,24},{12,26},{14,28},{16,30}... | collective-permute-start | bytes 98312 | tf_op jit(solution)/shard_map/ppermute | solution.py:64
  24.2 9.6 %collective-permute-start.7 = (f32[1,32,256]{2,1,0:T(8,128)S(1)}, f32[1,32,256]{2,1,0:T(8,128)S(1)}, u32[]{:S(2)}, u32[]{:S(2)}) collective-permute-start(f32[1,32,256]{2,1,0:T(8,128)S(1)} %bitcast.123), channel_id=1, source_target_pairs={{0,16},{2,18},{4,20},{6,22},{8,24},{10,26},{12,28},{14,30},{16,0},... | collective-permute-start | bytes 98312 | tf_op jit(solution)/shard_map/ppermute | solution.py:64
  25.5 8.4 %collective-permute-start.8 = (f32[1,32,256]{2,1,0:T(8,128)S(1)}, f32[1,32,256]{2,1,0:T(8,128)S(1)}, u32[]{:S(2)}, u32[]{:S(2)}) collective-permute-start(f32[1,32,256]{2,1,0:T(8,128)S(1)} %bitcast.122), channel_id=1, source_target_pairs={{0,18},{2,20},{4,22},{6,24},{8,26},{10,28},{12,30},{14,0},{16,2},{... | collective-permute-start | bytes 98312 | tf_op jit(solution)/shard_map/ppermute | solution.py:64
  26.4 8.8 %collective-permute-start.9 = (f32[1,32,256]{2,1,0:T(8,128)S(1)}, f32[1,32,256]{2,1,0:T(8,128)S(1)}, u32[]{:S(2)}, u32[]{:S(2)}) collective-permute-start(f32[1,32,256]{2,1,0:T(8,128)S(1)} %bitcast.121), channel_id=1, source_target_pairs={{0,20},{2,22},{4,24},{6,26},{8,28},{10,30},{12,0},{14,2},{16,4},{1... | collective-permute-start | bytes 98312 | tf_op jit(solution)/shard_map/ppermute | solution.py:64
  28.6 10.3 %collective-permute-start.10 = (f32[1,32,256]{2,1,0:T(8,128)S(1)}, f32[1,32,256]{2,1,0:T(8,128)S(1)}, u32[]{:S(2)}, u32[]{:S(2)}) collective-permute-start(f32[1,32,256]{2,1,0:T(8,128)S(1)} %bitcast.120), channel_id=1, source_target_pairs={{0,22},{2,24},{4,26},{6,28},{8,30},{10,0},{12,2},{14,4},{16,6},{18... | collective-permute-start | bytes 98312 | tf_op jit(solution)/shard_map/ppermute | solution.py:64
  31.8 7.2 %collective-permute-start.11 = (f32[1,32,256]{2,1,0:T(8,128)S(1)}, f32[1,32,256]{2,1,0:T(8,128)S(1)}, u32[]{:S(2)}, u32[]{:S(2)}) collective-permute-start(f32[1,32,256]{2,1,0:T(8,128)S(1)} %bitcast.119), channel_id=1, source_target_pairs={{0,24},{2,26},{4,28},{6,30},{8,0},{10,2},{12,4},{14,6},{16,8},{18,... | collective-permute-start | bytes 98312 | tf_op jit(solution)/shard_map/ppermute | solution.py:64
  33.8 5.8 %collective-permute-start.12 = (f32[1,32,256]{2,1,0:T(8,128)S(1)}, f32[1,32,256]{2,1,0:T(8,128)S(1)}, u32[]{:S(2)}, u32[]{:S(2)}) collective-permute-start(f32[1,32,256]{2,1,0:T(8,128)S(1)} %bitcast.118), channel_id=1, source_target_pairs={{0,26},{2,28},{4,30},{6,0},{8,2},{10,4},{12,6},{14,8},{16,10},{18,... | collective-permute-start | bytes 98312 | tf_op jit(solution)/shard_map/ppermute | solution.py:64
  33.9 5.7 %collective-permute-start.13 = (f32[1,32,256]{2,1,0:T(8,128)S(1)}, f32[1,32,256]{2,1,0:T(8,128)S(1)}, u32[]{:S(2)}, u32[]{:S(2)}) collective-permute-start(f32[1,32,256]{2,1,0:T(8,128)S(1)} %bitcast.117), channel_id=1, source_target_pairs={{0,28},{2,30},{4,0},{6,2},{8,4},{10,6},{12,8},{14,10},{16,12},{18,... | collective-permute-start | bytes 98312 | tf_op jit(solution)/shard_map/ppermute | solution.py:64
  35.2 5.5 %collective-permute-start.14 = (f32[1,32,256]{2,1,0:T(8,128)S(1)}, f32[1,32,256]{2,1,0:T(8,128)S(1)}, u32[]{:S(2)}, u32[]{:S(2)}) collective-permute-start(f32[1,32,256]{2,1,0:T(8,128)S(1)} %bitcast.116), channel_id=1, source_target_pairs={{0,30},{2,0},{4,2},{6,4},{8,6},{10,8},{12,10},{14,12},{16,14},{18,... | collective-permute-start | bytes 98312 | tf_op jit(solution)/shard_map/ppermute | solution.py:64
  40.7 23.6 %collective-permute-start.15 = (f32[512,256]{1,0:T(8,128)S(1)}, f32[512,256]{1,0:T(8,128)S(1)}, u32[]{:S(2)}, u32[]{:S(2)}) collective-permute-start(f32[512,256]{1,0:T(8,128)S(1)} %bitcast.104), channel_id=1, source_target_pairs={{0,30},{2,0},{4,2},{6,4},{8,6},{10,8},{12,10},{14,12},{16,14},{18,... | collective-permute-start | bytes 1572872 | tf_op jit(solution)/shard_map/ppermute | solution.py:28
  44.2 17.6 %collective-permute-start.19 = (f32[4]{0:T(128)S(1)}, f32[4]{0:T(128)S(1)}, u32[]{:S(2)}, u32[]{:S(2)}) collective-permute-start(f32[4]{0:T(128)S(1)} %select_reduce_fusion), channel_id=1, source_target_pairs={{0,30},{2,0},{4,2},{6,4},{8,6},{10,8},{12,10},{14,12},{16,14},{18,... | collective-permute-start | bytes 56 | tf_op jit(solution)/shard_map/ppermute | solution.py:28
  44.2 22.0 %collective-permute-start.17 = (f32[512,256]{1,0:T(8,128)S(1)}, f32[512,256]{1,0:T(8,128)S(1)}, u32[]{:S(2)}, u32[]{:S(2)}) collective-permute-start(f32[512,256]{1,0:T(8,128)S(1)} %bitcast.105), channel_id=1, source_target_pairs={{0,26},{2,28},{4,30},{6,0},{8,2},{10,4},{12,6},{14,8},{16,10},{18,... | collective-permute-start | bytes 1572872 | tf_op jit(solution)/shard_map/ppermute | solution.py:28
  70.0 1.0 copy-start
  71.1 20.3 %collective-permute-start.18 = (f32[256,512]{1,0:T(8,128)S(1)}, f32[256,512]{1,0:T(8,128)S(1)}, u32[]{:S(2)}, u32[]{:S(2)}) collective-permute-start(f32[256,512]{1,0:T(8,128)S(1)} %copy-done), channel_id=1, source_target_pairs={{0,26},{2,28},{4,30},{6,0},{8,2},{10,4},{12,6},{14,8},{16,10},{18,... | collective-permute-start | bytes 1572872 | tf_op jit(solution)/shard_map/ppermute | solution.py:28
  73.9 19.9 %collective-permute-start.16 = (f32[256,512]{1,0:T(8,128)S(1)}, f32[256,512]{1,0:T(8,128)S(1)}, u32[]{:S(2)}, u32[]{:S(2)}) collective-permute-start(f32[256,512]{1,0:T(8,128)S(1)} %copy-done), channel_id=1, source_target_pairs={{0,30},{2,0},{4,2},{6,4},{8,6},{10,8},{12,10},{14,12},{16,14},{18,... | collective-permute-start | bytes 1572872 | tf_op jit(solution)/shard_map/ppermute | solution.py:28
  89.9 1.4 copy-start.2
  91.4 1.9 %copy-start.3 = (f32[256,256]{1,0:T(8,128)S(1)}, f32[256,256]{1,0:T(8,128)}, u32[]{:S(2)}) copy-start(f32[256,256]{1,0:T(8,128)} %get-tuple-element.7) | copy-start | bytes 786436
  91.8 26.4 %collective-permute-start.20 = (f32[256,512]{1,0:T(8,128)S(1)}, f32[256,512]{1,0:T(8,128)S(1)}, u32[]{:S(2)}, u32[]{:S(2)}) collective-permute-start(f32[256,512]{1,0:T(8,128)S(1)} %convolution_add_fusion.5), channel_id=1, source_target_pairs={{0,2},{2,4},{4,6},{6,8},{8,10},{10,12},{12,14},{14,16},{16,18},{18... | collective-permute-start | bytes 1572872 | tf_op jit(solution)/shard_map/ppermute | solution.py:28
  93.7 2.9 %copy-start.6 = (f32[256,256]{1,0:T(8,128)S(1)}, f32[256,256]{1,0:T(8,128)}, u32[]{:S(2)}) copy-start(f32[256,256]{1,0:T(8,128)} %get-tuple-element.10) | copy-start | bytes 786436
  94.2 25.4 %collective-permute-start.21 = (f32[256,512]{1,0:T(8,128)S(1)}, f32[256,512]{1,0:T(8,128)S(1)}, u32[]{:S(2)}, u32[]{:S(2)}) collective-permute-start(f32[256,512]{1,0:T(8,128)S(1)} %convolution_add_fusion.4), channel_id=1, source_target_pairs={{0,6},{2,8},{4,10},{6,12},{8,14},{10,16},{12,18},{14,20},{16,22},{... | collective-permute-start | bytes 1572872 | tf_op jit(solution)/shard_map/ppermute | solution.py:28
  96.6 1.0 copy-start.1
  97.6 22.1 %copy-start.4 = (f32[256,512]{1,0:T(8,128)S(1)}, f32[256,512]{1,0:T(8,128)}, u32[]{:S(2)}) copy-start(f32[256,512]{1,0:T(8,128)} %param.12) | copy-start | bytes 1572868
  120.2 15.3 %collective-permute-start.23 = (f32[256,512]{1,0:T(8,128)S(1)}, f32[256,512]{1,0:T(8,128)S(1)}, u32[]{:S(2)}, u32[]{:S(2)}) collective-permute-start(f32[256,512]{1,0:T(8,128)S(1)} %fusion.6), channel_id=1, source_target_pairs={{0,26},{2,28},{4,30},{6,0},{8,2},{10,4},{12,6},{14,8},{16,10},{18,... | collective-permute-start | bytes 1572872 | tf_op jit(solution)/shard_map/ppermute | solution.py:28
  122.0 34.0 %collective-permute-start.22 = (f32[256,512]{1,0:T(8,128)S(1)}, f32[256,512]{1,0:T(8,128)S(1)}, u32[]{:S(2)}, u32[]{:S(2)}) collective-permute-start(f32[256,512]{1,0:T(8,128)S(1)} %fusion.6), channel_id=1, source_target_pairs={{0,30},{2,0},{4,2},{6,4},{8,6},{10,8},{12,10},{14,12},{16,14},{18,... | collective-permute-start | bytes 1572872 | tf_op jit(solution)/shard_map/ppermute | solution.py:28
  136.3 32.8 %collective-permute-start.24 = (f32[256,512]{1,0:T(8,128)S(1)}, f32[256,512]{1,0:T(8,128)S(1)}, u32[]{:S(2)}, u32[]{:S(2)}) collective-permute-start(f32[256,512]{1,0:T(8,128)S(1)} %convolution_add_fusion.1), channel_id=1, source_target_pairs={{0,2},{2,4},{4,6},{6,8},{8,10},{10,12},{12,14},{14,16},{16,18},{18... | collective-permute-start | bytes 1572872 | tf_op jit(solution)/shard_map/ppermute | solution.py:28
  156.8 16.1 %collective-permute-start.25 = (f32[256,512]{1,0:T(8,128)S(1)}, f32[256,512]{1,0:T(8,128)S(1)}, u32[]{:S(2)}, u32[]{:S(2)}) collective-permute-start(f32[256,512]{1,0:T(8,128)S(1)} %convolution_add_fusion), channel_id=1, source_target_pairs={{0,6},{2,8},{4,10},{6,12},{8,14},{10,16},{12,18},{14,20},{16,22},{... | collective-permute-start | bytes 1572872 | tf_op jit(solution)/shard_map/ppermute | solution.py:28
Sparse Core Ops, SparseCore 0:
  70.2 19.6 all-reduce.2
